TPU v7x, 128 devices: a whole 4x4x4 slice. The times are simulated.
128 devices in a mesh: section: 4 (over y), fsdp: 32 (over x, z, core).
Axes of the slice: x: 4, y: 4, z: 4, core: 2. Of those that a mesh axis runs over, the one named last changes fastest.
Arguments:
- inputs: bfloat16 [3, 128, 3072], P(None, 'fsdp'), may hold values from -6 to 6
- gain: float32 [4, 3072], P('section'), may hold values from 0.25 to 1.75
- w_gate: bfloat16 [4, 4, 3072, 8192], P('section', None, None, 'fsdp'), may hold values from -0.109375 to 0.109375
- w_up: bfloat16 [4, 4, 3072, 8192], P('section', None, None, 'fsdp'), may hold values from -0.109375 to 0.109375
- w_down: bfloat16 [4, 4, 8192, 3072], P('section', None, 'fsdp'), may hold values from -0.0625 to 0.0625
- routes: int32 [4, 3, 128, 2], P('section'), may hold values from 0 to 3, all different within a row
- shares: float32 [4, 3, 128, 2], P('section'), may hold values from 0.1 to 1
Outputs:
- hidden: bfloat16 [4, 3, 128, 3072], P('section', None, 'fsdp')
Inputs may be any that keep to these rules, and one draw needn't show every extreme that they name: `routes`: each token names 2 different experts, and every expert is named in each microbatch of each layer.
All inputs are finite; a program needn't handle non-finite values.
Results may differ from a plain program's by a relative error of at most 0.014.
Values may be sent and summed in bfloat16 or wider, within the bound.
A program may use at most 128 MiB of HBM per device.

v0:
```python
import jax
import jax.numpy as jnp
from jax import lax
from jax.sharding import PartitionSpec as P

BLOCK = 128


def passed_along(array, axis, by):
    devices = lax.axis_size(axis)
    pairs = [(i, i + by) for i in range(devices) if 0 <= i + by < devices]
    return lax.ppermute(array, axis, pairs)


def arrange(choices, experts, block, nblocks):
    flat_choice = choices.reshape(-1)
    slots_used = flat_choice.shape[0]
    onehot = (flat_choice[:, None] == jnp.arange(experts, dtype=jnp.int32)[None, :]).astype(
        jnp.int32
    )
    counts = jnp.sum(onehot, axis=0)
    padded = (counts + block - 1) // block * block
    ends = jnp.cumsum(padded)
    starts = ends - padded
    before = jnp.cumsum(onehot, axis=0) - onehot
    destination = jnp.sum((before + starts[None, :]) * onehot, axis=1)
    source = (
        jnp.zeros((nblocks * block,), jnp.int32)
        .at[destination]
        .set(jnp.arange(slots_used, dtype=jnp.int32))
    )
    slot_live = jnp.zeros((nblocks * block,), jnp.int32).at[destination].set(1)
    block_first = jnp.arange(nblocks, dtype=jnp.int32) * block
    block_expert = jnp.minimum(
        jnp.sum((block_first[:, None] >= ends[None, :]).astype(jnp.int32), axis=1), experts - 1
    )
    block_live = block_first < ends[experts - 1]
    return (destination, source, slot_live, block_expert, block_live)


def rms_norm(rows, gain_row):
    values = rows.astype(jnp.float32)
    scale = lax.rsqrt(jnp.mean(values * values, axis=-1, keepdims=True) + 1e-05)
    return (values * scale * gain_row[None, :]).astype(jnp.bfloat16)


def expert_mix(normed, choices, weights_share, gate_w, up_w, down_w):
    tokens, width = normed.shape
    experts = gate_w.shape[0]
    nblocks = (2 * tokens + BLOCK - 1) // BLOCK + experts
    destination, source, slot_live, block_expert, block_live = arrange(
        choices, experts, BLOCK, nblocks
    )
    picked_rows = jnp.where(
        slot_live[:, None] > 0, normed[source // 2], jnp.zeros((), normed.dtype)
    )
    blocks = picked_rows.reshape(nblocks, BLOCK, width)

    def compute(operand, expert_id):
        gate = jnp.dot(operand, gate_w[expert_id], preferred_element_type=jnp.float32)
        upward = jnp.dot(operand, up_w[expert_id], preferred_element_type=jnp.float32)
        gated = (jax.nn.silu(gate) * upward).astype(jnp.bfloat16)
        return jnp.dot(gated, down_w[expert_id], preferred_element_type=jnp.float32)

    def one_block(carry, item):
        rows_block, expert_id, live = item
        result = compute(rows_block, expert_id)
        return (carry, result)

    _, results = lax.scan(one_block, jnp.zeros((), jnp.int32), (blocks, block_expert, block_live))
    results = results.reshape(nblocks * BLOCK, width)
    chosen = results[destination].reshape(tokens, 2, width)
    return jnp.sum(chosen * weights_share[:, :, None], axis=1)


def on_device(inputs, gain, w_gate, w_up, w_down, routes, shares):
    sections = lax.axis_size("section")
    section_index = lax.axis_index("section")
    micro_count = inputs.shape[0]
    local_rows = inputs.shape[1]
    width = inputs.shape[2]
    gain_row = gain[0]
    gate_w = w_gate[0]
    up_w = w_up[0]
    down_w = w_down[0]
    route_layer = routes[0]
    share_layer = shares[0]
    outputs = jnp.zeros((micro_count, local_rows, width), jnp.bfloat16)
    carried = None
    total_ticks = micro_count + sections - 1
    for tick in range(total_ticks):
        position = tick - section_index
        valid = jnp.logical_and(position >= 0, position < micro_count)
        clipped = jnp.clip(position, 0, micro_count - 1)
        route_micro = lax.dynamic_index_in_dim(route_layer, clipped, 0, keepdims=False)
        share_micro = lax.dynamic_index_in_dim(share_layer, clipped, 0, keepdims=False)
        entry = lax.dynamic_index_in_dim(inputs, clipped, 0, keepdims=False)
        if carried is None:
            current = entry
        else:
            current = jnp.where(section_index == 0, entry, carried)
        normed = rms_norm(current, gain_row)
        gathered = lax.all_gather(normed, "fsdp", axis=0, tiled=True)
        partial_value = expert_mix(gathered, route_micro, share_micro, gate_w, up_w, down_w)
        mixed = lax.psum_scatter(partial_value, "fsdp", scatter_dimension=0, tiled=True)
        result = (current.astype(jnp.float32) + mixed).astype(jnp.bfloat16)
        if tick + 1 < total_ticks:
            carried = passed_along(result, "section", 1)
        updated = lax.dynamic_update_index_in_dim(outputs, result, clipped, 0)
        outputs = jnp.where(valid, updated, outputs)
    return outputs[None]


def solution(mesh):
    placed = (
        P(None, "fsdp", None),
        P("section", None),
        P("section", None, None, "fsdp"),
        P("section", None, None, "fsdp"),
        P("section", None, "fsdp", None),
        P("section", None, None, None),
        P("section", None, None, None),
    )
    return jax.shard_map(
        on_device,
        mesh=mesh,
        in_specs=placed,
        out_specs=P("section", None, "fsdp", None),
        check_vma=False,
    )
```

profile of v0, /device:TPU:24, one launch (start us, length us, event | category | flops | bytes accessed | tf_op | source)
XLA Modules:
  0.0 1363.1 jit_solution(5283009128699849334)
XLA Ops:
  15.5 26.2 %all-gather = bf16[32,4,3072]{2,1,0:T(4,128)(2,1)S(1)} all-gather(bf16[1,4,3072]{2,1,0:T(4,128)(2,1)S(1)} %fusion.222), channel_id=1, replica_groups=mesh['section'=4,'fsdp'=32] {'fsdp'}, dimensions={0}, use_global_device_ids=true | all-gather | bytes 811008 | tf_op jit(solution)/shard_map/all_gather | solution.py:103
  47.8 4.9 gather_fusion
  52.8 5.0 broadcast_select_fusion.5
  58.9 4.8 broadcast.973.clone
  63.7 53.3 %while.60 = (s32[]{:T(128)}, f32[6,128,3072]{2,1,0:T(8,128)}, bf16[6,128,3072]{2,1,0:T(8,128)(2,1)}, s32[6]{0:T(128)S(1)}, bf16[4,3072,256]{2,1,0:T(8,128)(2,1)}...) while((s32[]{:T(128)}, f32[6,128,3072]{2,1,0:T(8,128)}, ...), condition=%wide.region_10.11_spmd, body=%wide.region_9.10_spmd.sunk | while | flops 604176384 | bytes 8129175 | solution.py:70
  68.3 4.3 fusion.355
  94.9 4.3 fusion.355
  112.7 4.4 fusion.355
  117.1 8.3 gather_fusion.1
  130.7 6.4 multiply_reduce_fusion.5
  152.8 89.9 %all-reduce.13.cloned.1.call-done = f32[128,3072]{1,0:T(8,128)} async-done(((f32[128,3072]{1,0:T(8,128)}), f32[128,3072]{1,0:T(8,128)}) %all-reduce.13.cloned.1.call-update) | async-done | bytes 1572880
  249.7 25.3 %all-gather.1 = bf16[32,4,3072]{2,1,0:T(4,128)(2,1)S(1)} all-gather(bf16[1,4,3072]{2,1,0:T(4,128)(2,1)S(1)} %fusion.231), channel_id=1, replica_groups=mesh['section'=4,'fsdp'=32] {'fsdp'}, dimensions={0}, use_global_device_ids=true | all-gather | bytes 811008 | tf_op jit(solution)/shard_map/all_gather | solution.py:103
  275.2 5.4 gather_fusion.2
  280.6 5.0 broadcast_select_fusion.4
  285.5 4.8 broadcast.973.clone.1
  290.3 51.9 %while.61 = (s32[]{:T(128)}, f32[6,128,3072]{2,1,0:T(8,128)}, bf16[6,128,3072]{2,1,0:T(8,128)(2,1)}, s32[6]{0:T(128)S(1)}, bf16[4,3072,256]{2,1,0:T(8,128)(2,1)}...) while((s32[]{:T(128)}, f32[6,128,3072]{2,1,0:T(8,128)}, ...), condition=%wide.region_23.24_spmd, body=%wide.region_22.23_spmd.sunk | while | flops 604176384 | bytes 8129175 | solution.py:70
  294.7 4.3 fusion.362
  320.6 4.3 fusion.362
  337.9 4.4 fusion.362
  342.3 8.3 gather_fusion.3
  354.4 5.5 multiply_reduce_fusion.4
  361.8 102.9 %all-reduce.15.cloned.1.call-done = f32[128,3072]{1,0:T(8,128)} async-done(((f32[128,3072]{1,0:T(8,128)}), f32[128,3072]{1,0:T(8,128)}) %all-reduce.15.cloned.1.call-update) | async-done | bytes 1572880
  471.8 25.3 %all-gather.2 = bf16[32,4,3072]{2,1,0:T(4,128)(2,1)S(1)} all-gather(bf16[1,4,3072]{2,1,0:T(4,128)(2,1)S(1)} %fusion.230), channel_id=1, replica_groups=mesh['section'=4,'fsdp'=32] {'fsdp'}, dimensions={0}, use_global_device_ids=true | all-gather | bytes 811008 | tf_op jit(solution)/shard_map/all_gather | solution.py:103
  497.4 5.1 gather_fusion.4
  502.5 5.0 broadcast_select_fusion.3
  507.4 4.8 broadcast.973.clone.2
  512.2 51.9 %while.62 = (s32[]{:T(128)}, f32[6,128,3072]{2,1,0:T(8,128)}, bf16[6,128,3072]{2,1,0:T(8,128)(2,1)}, s32[6]{0:T(128)S(1)}, bf16[4,3072,256]{2,1,0:T(8,128)(2,1)}...) while((s32[]{:T(128)}, f32[6,128,3072]{2,1,0:T(8,128)}, ...), condition=%wide.region_36.37_spmd, body=%wide.region_35.36_spmd.sunk | while | flops 604176384 | bytes 8129175 | solution.py:70
  542.4 4.3 fusion.369
  559.7 4.4 fusion.369
  564.1 8.3 gather_fusion.5
  576.2 5.5 multiply_reduce_fusion.3
  581.9 106.4 %all-reduce.17.cloned.1.call-done = f32[128,3072]{1,0:T(8,128)} async-done(((f32[128,3072]{1,0:T(8,128)}), f32[128,3072]{1,0:T(8,128)}) %all-reduce.17.cloned.1.call-update) | async-done | bytes 1572880
  695.2 25.3 %all-gather.3 = bf16[32,4,3072]{2,1,0:T(4,128)(2,1)S(1)} all-gather(bf16[1,4,3072]{2,1,0:T(4,128)(2,1)S(1)} %fusion.229), channel_id=1, replica_groups=mesh['section'=4,'fsdp'=32] {'fsdp'}, dimensions={0}, use_global_device_ids=true | all-gather | bytes 811008 | tf_op jit(solution)/shard_map/all_gather | solution.py:103
  720.7 5.4 gather_fusion.6
  726.1 5.0 broadcast_select_fusion.2
  731.0 4.8 broadcast.973.clone.3
  735.8 51.9 %while.63 = (s32[]{:T(128)}, f32[6,128,3072]{2,1,0:T(8,128)}, bf16[6,128,3072]{2,1,0:T(8,128)(2,1)}, s32[6]{0:T(128)S(1)}, bf16[4,3072,256]{2,1,0:T(8,128)(2,1)}...) while((s32[]{:T(128)}, f32[6,128,3072]{2,1,0:T(8,128)}, ...), condition=%wide.region_49.50_spmd, body=%wide.region_48.49_spmd.sunk | while | flops 604176384 | bytes 8129175 | solution.py:70
  740.2 4.3 fusion.376
  766.0 4.3 fusion.376
  783.3 4.4 fusion.376
  787.7 8.3 gather_fusion.7
  799.8 5.5 multiply_reduce_fusion.2
  808.6 101.5 %all-reduce.19.cloned.1.call-done = f32[128,3072]{1,0:T(8,128)} async-done(((f32[128,3072]{1,0:T(8,128)}), f32[128,3072]{1,0:T(8,128)}) %all-reduce.19.cloned.1.call-update) | async-done | bytes 1572880
  917.0 25.3 %all-gather.4 = bf16[32,4,3072]{2,1,0:T(4,128)(2,1)S(1)} all-gather(bf16[1,4,3072]{2,1,0:T(4,128)(2,1)S(1)} %fusion.228), channel_id=1, replica_groups=mesh['section'=4,'fsdp'=32] {'fsdp'}, dimensions={0}, use_global_device_ids=true | all-gather | bytes 811008 | tf_op jit(solution)/shard_map/all_gather | solution.py:103
  942.5 5.0 gather_fusion.8
  947.5 5.0 broadcast_select_fusion.1
  952.4 4.8 broadcast.973.clone.4
  957.2 51.9 %while.64 = (s32[]{:T(128)}, f32[6,128,3072]{2,1,0:T(8,128)}, bf16[6,128,3072]{2,1,0:T(8,128)(2,1)}, s32[6]{0:T(128)S(1)}, bf16[4,3072,256]{2,1,0:T(8,128)(2,1)}...) while((s32[]{:T(128)}, f32[6,128,3072]{2,1,0:T(8,128)}, ...), condition=%wide.region_62.63_spmd, body=%wide.region_61.62_spmd.sunk | while | flops 604176384 | bytes 8129175 | solution.py:70
  987.4 4.3 fusion.383
  1004.7 4.4 fusion.383
  1009.1 8.3 gather_fusion.9
  1021.2 5.5 multiply_reduce_fusion.1
  1030.0 101.5 %all-reduce.21.cloned.1.call-done = f32[128,3072]{1,0:T(8,128)} async-done(((f32[128,3072]{1,0:T(8,128)}), f32[128,3072]{1,0:T(8,128)}) %all-reduce.21.cloned.1.call-update) | async-done | bytes 1572880
  1138.4 25.3 %all-gather.5 = bf16[32,4,3072]{2,1,0:T(4,128)(2,1)S(1)} all-gather(bf16[1,4,3072]{2,1,0:T(4,128)(2,1)S(1)} %fusion.227), channel_id=1, replica_groups=mesh['section'=4,'fsdp'=32] {'fsdp'}, dimensions={0}, use_global_device_ids=true | all-gather | bytes 811008 | tf_op jit(solution)/shard_map/all_gather | solution.py:103
  1163.9 5.0 gather_fusion.10
  1168.9 5.0 broadcast_select_fusion
  1173.8 4.8 broadcast.973
  1178.6 53.4 %while.65 = (s32[]{:T(128)}, f32[6,128,3072]{2,1,0:T(8,128)}, bf16[6,128,3072]{2,1,0:T(8,128)(2,1)}, s32[6]{0:T(128)S(1)}, bf16[4,3072,256]{2,1,0:T(8,128)(2,1)}...) while((s32[]{:T(128)}, f32[6,128,3072]{2,1,0:T(8,128)}, ...), condition=%wide.region_75.76_spmd, body=%wide.region_74.75_spmd.sunk | while | flops 604176384 | bytes 8129175 | solution.py:70
  1183.2 4.3 fusion.390
  1209.8 4.3 fusion.390
  1227.6 4.4 fusion.390
  1232.0 8.3 gather_fusion.11
  1244.1 5.5 multiply_reduce_fusion
  1250.2 104.2 %all-reduce.23.cloned.1.call-done = f32[128,3072]{1,0:T(8,128)} async-done(((f32[128,3072]{1,0:T(8,128)}), f32[128,3072]{1,0:T(8,128)}) %all-reduce.23.cloned.1.call-update) | async-done | bytes 1572880
  (350 shorter events, 282.2 us)
Async XLA Ops:
  6.5 236.2 %all-reduce.13.cloned.1.call-start = ((), (), s32[]{:S(2)}) async-start(), calls=%async_computation | async-start | bytes 3145728
  41.9 10.9 copy-start.16
  44.1 0.5 copy-start.17
  44.9 12.9 copy-start.9
  45.3 0.6 copy-start.18
  45.5 12.3 copy-start.11
  46.2 0.6 copy-start.20
  46.4 11.3 copy-start.14
  47.0 0.6 copy-start.19
  47.8 9.9 copy-start.13
  125.4 3.9 copy-start.2
  129.3 7.9 copy-start.12
  129.3 9.5 copy-start.10
  129.3 113.4 %copy-start = (bf16[3,4,3072]{2,1,0:T(4,128)(2,1)S(1)}, bf16[3,4,3072]{2,1,0:T(4,128)(2,1)}, u32[]{:S(2)}) copy-start(bf16[3,4,3072]{2,1,0:T(4,128)(2,1)} %param.19) | copy-start | bytes 221188
  129.3 120.2 %copy-start.1 = (f32[1,3072]{1,0:T(1,128)S(1)}, f32[1,3072]{1,0:T(1,128)}, u32[]{:S(2)}) copy-start(f32[1,3072]{1,0:T(1,128)} %param.20) | copy-start | bytes 36868
  130.0 8.1 copy-start.15
  137.1 327.5 %all-reduce.15.cloned.1.call-start = ((), (), s32[]{:S(2)}) async-start(), calls=%async_computation.1 | async-start | bytes 3145728
  243.7 5.7 collective-permute-start
  285.5 4.8 copy-start.6
  354.3 7.3 copy-start.8
  354.3 7.4 copy-start.4
  354.4 7.4 copy-start.5
  359.9 328.4 %all-reduce.17.cloned.1.call-start = ((), (), s32[]{:S(2)}) async-start(), calls=%async_computation.2 | async-start | bytes 3145728
  465.6 6.0 collective-permute-start.1
  576.2 5.6 copy-start.7
  581.7 328.4 %all-reduce.19.cloned.1.call-start = ((), (), s32[]{:S(2)}) async-start(), calls=%async_computation.3 | async-start | bytes 3145728
  689.2 5.7 collective-permute-start.2
  805.3 326.2 %all-reduce.21.cloned.1.call-start = ((), (), s32[]{:S(2)}) async-start(), calls=%async_computation.4 | async-start | bytes 3145728
  911.0 5.7 collective-permute-start.3
  1021.1 112.6 %copy-start.3 = (f32[128,2]{0,1:T(2,128)S(1)}, f32[128,2]{0,1:T(2,128)}, u32[]{:S(2)}) copy-start(f32[128,2]{0,1:T(2,128)} %get-tuple-element.343) | copy-start | bytes 3076
  1026.7 327.7 %all-reduce.23.cloned.1.call-start = ((), (), s32[]{:S(2)}) async-start(), calls=%async_computation.5 | async-start | bytes 3145728
  1132.4 5.7 collective-permute-start.4
Sparse Core Ops, SparseCore 0:
  137.3 105.4 all-reduce.12
  360.0 104.6 all-reduce.14
  581.8 106.4 all-reduce.16
  805.4 104.6 all-reduce.18
  1026.8 104.6 all-reduce.20
  1249.7 104.6 all-reduce.22
where the time goes:
time: 1370 us; the launch traced here: 1360 us
  waiting for transfers between devices  624 us (46%)
  matrix products  230 us (17%)
  local copies, waits for them, and re-layouts  183 us (13%)
  blocking collectives  153 us (11%)
  other arithmetic  88.3 us (6%)
  loops' own time  63.4 us (5%)
  between operations  15.4 us (1%)
    unnamed x12, waiting for transfers between devices  606 us
    dot_general x36, matrix products, compute(): return jnp.dot(gated, down_w[expert_id], preferred_element_type=jnp.float32)  156 us
    all_gather x6, blocking collectives, on_device(): gathered = lax.all_gather(normed, 'fsdp', axis=0, tiled=True)  153 us
    dot_general x36, matrix products, compute(): jnp.dot(operand, gate_w[expert_id], preferred_element_type=jnp.float32)  73.3 us
    another operation x6, loops' own time, expert_mix(): lax.scan(one_block, jnp.zeros((), jnp.int32), (blocks, block_expert, bloc...  63.4 us
    gather x6, local copies, waits for them, and re-layouts, expert_mix(): chosen = results[destination].reshape(tokens, 2, width)  49.9 us
    reduce_sum x6, other arithmetic, expert_mix(): return jnp.sum(chosen * weights_share[:, :, None], axis=1)  33.8 us
    gather x6, local copies, waits for them, and re-layouts, expert_mix(): normed[source // 2]  30.7 us
  transfers between devices with their start and end apart: 11, of which 10 were waited for; matrix products, arithmetic and copies ran while one was open for 2% of the time, Pallas kernels for 0%

commit v1 on v0

v1 whole, which is shorter than its diff:
```python
import jax
import jax.numpy as jnp
from jax import lax
from jax.sharding import PartitionSpec as P


def passed_along(array, axis, by):
    devices = lax.axis_size(axis)
    pairs = [(i, i + by) for i in range(devices) if 0 <= i + by < devices]
    return lax.ppermute(array, axis, pairs)


def rms_norm(rows, gain_row):
    values = rows.astype(jnp.float32)
    scale = lax.rsqrt(jnp.mean(values * values, axis=-1, keepdims=True) + 1e-05)
    return (values * scale * gain_row[None, :]).astype(jnp.bfloat16)


def combine_weights(route_layer, share_layer, experts, shards):
    micro, tokens, top = route_layer.shape
    per = tokens // shards
    onehot = (route_layer[..., None] == jnp.arange(experts, dtype=route_layer.dtype)).astype(jnp.float32)
    coef = jnp.sum(onehot * share_layer[..., None], axis=2)
    coef = coef.reshape(micro, shards, per, experts).transpose(3, 1, 0, 2)
    return coef.reshape(experts, shards, micro * per)


def expert_mix(rows, coef, gate_w, up_w, down_w):
    gate = jnp.einsum("fmd,edh->efmh", rows, gate_w, preferred_element_type=jnp.float32)
    upward = jnp.einsum("fmd,edh->efmh", rows, up_w, preferred_element_type=jnp.float32)
    gated = (jax.nn.silu(gate) * upward * coef[..., None]).astype(jnp.bfloat16)
    return jnp.einsum("efmh,ehd->fmd", gated, down_w, preferred_element_type=jnp.float32)


def on_device(inputs, gain, w_gate, w_up, w_down, routes, shares):
    sections = lax.axis_size("section")
    shards = lax.axis_size("fsdp")
    section_index = lax.axis_index("section")
    micro, local, width = inputs.shape
    gain_row = gain[0]
    gate_w, up_w, down_w = w_gate[0], w_up[0], w_down[0]
    coef = combine_weights(routes[0], shares[0], gate_w.shape[0], shards)
    current = inputs.reshape(micro * local, width)
    output = jnp.zeros_like(current)
    for tick in range(sections):
        if tick > 0:
            current = passed_along(result, "section", 1)
        normed = rms_norm(current, gain_row)
        gathered = lax.all_gather(normed, "fsdp", axis=0, tiled=False)
        partial_value = expert_mix(gathered, coef, gate_w, up_w, down_w)
        mixed = lax.psum_scatter(partial_value, "fsdp", scatter_dimension=0, tiled=True)[0]
        result = (current.astype(jnp.float32) + mixed).astype(jnp.bfloat16)
        output = jnp.where(section_index == tick, result, output)
    return output.reshape(1, micro, local, width)


def solution(mesh):
    placed = (
        P(None, "fsdp", None),
        P("section", None),
        P("section", None, None, "fsdp"),
        P("section", None, None, "fsdp"),
        P("section", None, "fsdp", None),
        P("section", None, None, None),
        P("section", None, None, None),
    )
    return jax.shard_map(
        on_device,
        mesh=mesh,
        in_specs=placed,
        out_specs=P("section", None, "fsdp", None),
        check_vma=False,
    )
```

time: 1370 us -> 762 us (0.56)
  local copies, waits for them, and re-layouts: 183 us -> 11.5 us
  blocking collectives: 153 us -> 0 us
  matrix products: 230 us -> 81.4 us
  other arithmetic: 88.3 us -> 5.97 us
  loops' own time: 63.4 us -> 0 us
  waiting for transfers between devices: 624 us -> 643 us
    all_gather x0 -> x4, waiting for transfers between devices: none -> 180 us  [on_device(): gathered = lax.all_gather(normed, 'fsdp', axis=0, tiled=False)]
    unnamed x12, waiting for transfers between devices: 606 us -> 448 us
    all_gather x6 -> x0, blocking collectives: 153 us -> none  [on_device(): gathered = lax.all_gather(normed, 'fsdp', axis=0, tiled=True)]
    dot_general x72 -> x8, matrix products: 230 us -> 81.4 us  [the longest x4 53.3 us: expert_mix(): jnp.einsum('efmh,ehd->fmd', gated, down_w, preferred_element_type=jnp.flo...]
    gather x12 -> x0, local copies, waits for them, and re-layouts: 80.6 us -> none  [the longest x6 49.9 us: expert_mix(): chosen = results[destination].reshape(tokens, 2, width)]
    another operation x6 -> x0, loops' own time: 63.4 us -> none  [expert_mix(): lax.scan(one_block, jnp.zeros((), jnp.int32), (blocks, block_expert, bloc...]
    select_n x21 -> x1, other arithmetic: 36 us -> 0.05 us  [on_device(): output = jnp.where(section_index == tick, result, output)]
    reduce_sum x19 -> x1, other arithmetic: 35.7 us -> 0.73 us  [combine_weights(): coef = jnp.sum(onehot * share_layer[..., None], axis=2)]
  transfers between devices with their start and end apart: 11 -> 11, of which waited for: 10 -> 11; matrix products, arithmetic and copies ran while one was open for 2% -> 0% of each run, Pallas kernels for 0% -> 0%
where the time goes in v1:
time: 762 us; the launch traced here: 761 us
  waiting for transfers between devices  643 us (84%)
  matrix products  81.4 us (11%)
  between operations  13.6 us (2%)
  local copies, waits for them, and re-layouts  11.5 us (2%)
    unnamed x12, waiting for transfers between devices  448 us
    all_gather x4, waiting for transfers between devices, on_device(): gathered = lax.all_gather(normed, 'fsdp', axis=0, tiled=False)  180 us
    dot_general x4, matrix products, expert_mix(): jnp.einsum('efmh,ehd->fmd', gated, down_w, preferred_element_type=jnp.flo...  53.3 us
    dot_general x4, matrix products, expert_mix(): jnp.einsum('fmd,edh->efmh', rows, gate_w, preferred_element_type=jnp.floa...  28.1 us
    ppermute x3, waiting for transfers between devices, passed_along(): return lax.ppermute(array, axis, pairs)  15.6 us
  transfers between devices with their start and end apart: 11, of which 11 were waited for; matrix products, arithmetic and copies ran while one was open for 0% of the time, Pallas kernels for 0%

profile of v1, /device:TPU:24, one launch (start us, length us, event | category | flops | bytes accessed | tf_op | source)
XLA Modules:
  0.0 760.8 jit_solution(1780995400904305538)
XLA Ops:
  6.5 0.0 all-gather.11.cloned.1.call-start
  6.5 0.9 reshape.120
  7.4 1.0 multiply_reduce_fusion
  8.5 0.1 rsqrt.36
  8.5 1.4 multiply_convert_fusion
  10.0 0.0 all-gather.11.cloned.1.call-update
  10.0 0.0 all-reduce.9.cloned.1.call-start
  10.1 0.7 select_reduce_fusion
  10.8 0.2 reshape.117
  11.0 0.1 copy.98
  11.1 46.3 %all-gather.11.cloned.1.call-done = bf16[32,12,3072]{2,1,0:T(8,128)(2,1)} async-done(((bf16[1,12,3072]{2,1,0:T(8,128)(2,1)}), bf16[32,12,3072]{2,1,0:T(8,128)(2,1)}) %all-gather.11.cloned.1.call-update) | async-done | bytes 2359312 | tf_op jit(solution)/shard_map/all_gather | solution.py:49
  57.4 0.0 copy-start.2
  57.5 8.0 %fusion.22 = f32[32,12,4,256]{3,0,2,1:T(8,128)} fusion(bf16[1,4,3072,256]{3,2,1,0:T(8,128)(2,1)} %param.9, bf16[32,12,3072,1]{2,1,0,3:T(8,128)(2,1)} %bitcast.203), kind=kOutput, calls=%fused_computation.22 | convolution fusion | flops 2415919104 | bytes 10223616 | tf_op jit(solution)/shard_map/fmd,edh->efmh/dot_general | solution.py:29
  65.5 0.0 copy-done.2
  65.5 13.4 %fusion.24 = f32[32,12,3072]{2,0,1:T(8,128)} fusion(bf16[1,4,256,3072]{3,2,1,0:T(8,128)(2,1)} %param.11, f32[32,12,4,256]{3,0,2,1:T(8,128)} %fusion.22, bf16[1,4,3072,256]{3,2,1,0:T(8,128)(2,1)} %param.10, bf16[32,12,3072,1]{2,1,0,3:T(8,128)(2,1)S(1)} %bitcast.204, f32[4,32,12]{1,0,2:T(4,128)S(1)} %bitcast.197), kind=kOutput, calls=%fused_computation.24 | convolution fusion | flops 4834590720 | bytes 21239808 | tf_op jit(solution)/shard_map/efmh,ehd->fmd/dot_general | solution.py:32
  78.8 0.0 all-reduce.9.cloned.1.call-update
  78.8 0.0 all-gather.13.cloned.1.call-start
  78.9 0.8 copy-done
  79.7 0.0 copy-done.4
  79.7 0.6 dynamic-slice
  80.3 110.6 %all-reduce.9.cloned.1.call-done = f32[32,12,3072]{2,0,1:T(8,128)} async-done(((f32[32,12,3072]{2,0,1:T(8,128)}), f32[32,12,3072]{2,0,1:T(8,128)}) %all-reduce.9.cloned.1.call-update) | async-done | bytes 4718608
  190.9 2.0 constant_dynamic-slice_fusion.3
  193.0 1.3 collective-permute-start
  194.3 5.2 collective-permute-done
  199.5 0.1 fusion.104
  199.7 0.0 copy-done.1
  199.7 0.7 fusion.120
  200.4 0.0 all-gather.13.cloned.1.call-update
  200.4 0.2 all-reduce.11.cloned.1.call-start
  200.7 44.7 %all-gather.13.cloned.1.call-done = bf16[32,12,3072]{2,1,0:T(8,128)(2,1)} async-done(((bf16[1,12,3072]{2,1,0:T(8,128)(2,1)}), bf16[32,12,3072]{2,1,0:T(8,128)(2,1)}) %all-gather.13.cloned.1.call-update) | async-done | bytes 2359312 | tf_op jit(solution)/shard_map/all_gather | solution.py:49
  245.3 8.0 %fusion.20 = f32[32,12,4,256]{3,0,2,1:T(8,128)} fusion(bf16[1,4,3072,256]{3,2,1,0:T(8,128)(2,1)} %param.9, bf16[32,12,3072,1]{2,1,0,3:T(8,128)(2,1)} %bitcast.207), kind=kOutput, calls=%fused_computation.20 | convolution fusion | flops 2415919104 | bytes 10223616 | tf_op jit(solution)/shard_map/fmd,edh->efmh/dot_general | solution.py:29
  253.4 0.0 copy-done.3
  253.4 13.4 %fusion.27 = f32[32,12,3072]{2,0,1:T(8,128)} fusion(bf16[1,4,256,3072]{3,2,1,0:T(8,128)(2,1)} %param.11, f32[32,12,4,256]{3,0,2,1:T(8,128)} %fusion.20, bf16[1,4,3072,256]{3,2,1,0:T(8,128)(2,1)} %param.10, bf16[32,12,3072,1]{2,1,0,3:T(8,128)(2,1)S(1)} %bitcast.208, f32[4,32,12]{1,0,2:T(4,128)S(1)} %bitcast.198), kind=kOutput, calls=%fused_computation.25 | convolution fusion | flops 4834590720 | bytes 21239808 | tf_op jit(solution)/shard_map/efmh,ehd->fmd/dot_general | solution.py:32
  266.7 0.0 all-reduce.11.cloned.1.call-update
  266.8 0.0 all-gather.15.cloned.1.call-start
  266.8 112.2 %all-reduce.11.cloned.1.call-done = f32[32,12,3072]{2,0,1:T(8,128)} async-done(((f32[32,12,3072]{2,0,1:T(8,128)}), f32[32,12,3072]{2,0,1:T(8,128)}) %all-reduce.11.cloned.1.call-update) | async-done | bytes 4718608
  379.0 2.0 constant_dynamic-slice_fusion.2
  381.1 1.3 collective-permute-start.1
  382.4 5.2 collective-permute-done.1
  387.6 0.1 fusion.108
  387.8 0.7 fusion.119
  388.5 0.0 all-gather.15.cloned.1.call-update
  388.5 0.3 all-reduce.13.cloned.1.call-start
  388.8 44.6 %all-gather.15.cloned.1.call-done = bf16[32,12,3072]{2,1,0:T(8,128)(2,1)} async-done(((bf16[1,12,3072]{2,1,0:T(8,128)(2,1)}), bf16[32,12,3072]{2,1,0:T(8,128)(2,1)}) %all-gather.15.cloned.1.call-update) | async-done | bytes 2359312 | tf_op jit(solution)/shard_map/all_gather | solution.py:49
  433.4 6.0 fusion.18
  439.4 13.3 %fusion.30 = f32[32,12,3072]{2,0,1:T(8,128)} fusion(bf16[1,4,256,3072]{3,2,1,0:T(8,128)(2,1)} %param.11, f32[32,12,4,256]{3,0,2,1:T(8,128)S(1)} %fusion.18, bf16[1,4,3072,256]{3,2,1,0:T(8,128)(2,1)} %param.10, bf16[32,12,3072,1]{2,1,0,3:T(8,128)(2,1)} %bitcast.210, f32[4,32,12]{1,0,2:T(4,128)S(1)} %bitcast.199), kind=kOutput, calls=%fused_computation.26 | convolution fusion | flops 4834590720 | bytes 21239808 | tf_op jit(solution)/shard_map/efmh,ehd->fmd/dot_general | solution.py:32
  452.8 0.0 all-reduce.13.cloned.1.call-update
  452.8 0.0 all-gather.17.cloned.1.call-start
  452.9 112.2 %all-reduce.13.cloned.1.call-done = f32[32,12,3072]{2,0,1:T(8,128)} async-done(((f32[32,12,3072]{2,0,1:T(8,128)}), f32[32,12,3072]{2,0,1:T(8,128)}) %all-reduce.13.cloned.1.call-update) | async-done | bytes 4718608
  565.1 2.0 constant_dynamic-slice_fusion.1
  567.1 1.3 collective-permute-start.2
  568.4 5.2 collective-permute-done.2
  573.6 0.1 fusion.112
  573.8 0.7 fusion.118
  574.5 0.0 all-gather.17.cloned.1.call-update
  574.5 0.3 all-reduce.15.cloned.1.call-start
  574.9 44.6 %all-gather.17.cloned.1.call-done = bf16[32,12,3072]{2,1,0:T(8,128)(2,1)} async-done(((bf16[1,12,3072]{2,1,0:T(8,128)(2,1)}), bf16[32,12,3072]{2,1,0:T(8,128)(2,1)}) %all-gather.17.cloned.1.call-update) | async-done | bytes 2359312 | tf_op jit(solution)/shard_map/all_gather | solution.py:49
  619.5 6.0 fusion.16
  625.5 13.3 %fusion.33 = f32[32,12,3072]{2,0,1:T(8,128)} fusion(bf16[1,4,256,3072]{3,2,1,0:T(8,128)(2,1)} %param.11, f32[32,12,4,256]{3,0,2,1:T(8,128)S(1)} %fusion.16, bf16[1,4,3072,256]{3,2,1,0:T(8,128)(2,1)} %param.10, bf16[32,12,3072,1]{2,1,0,3:T(8,128)(2,1)} %bitcast.206, f32[4,32,12]{1,0,2:T(4,128)S(1)} %bitcast.200), kind=kOutput, calls=%fused_computation.27 | convolution fusion | flops 4834590720 | bytes 21239808 | tf_op jit(solution)/shard_map/efmh,ehd->fmd/dot_general | solution.py:32
  638.8 0.0 all-reduce.15.cloned.1.call-update
  638.8 112.4 %all-reduce.15.cloned.1.call-done = f32[32,12,3072]{2,0,1:T(8,128)} async-done(((f32[32,12,3072]{2,0,1:T(8,128)}), f32[32,12,3072]{2,0,1:T(8,128)}) %all-reduce.15.cloned.1.call-update) | async-done | bytes 4718608
  751.2 2.0 constant_dynamic-slice_fusion
  753.3 0.1 fusion.117
  753.3 0.7 reshape.118
  (12 shorter events, 0.2 us)
Async XLA Ops:
  6.5 50.9 %all-gather.11.cloned.1.call-start = ((), (), s32[]{:S(2)}) async-start(), calls=%async_computation | async-start | bytes 3244032 | tf_op jit(solution)/shard_map/all_gather | solution.py:49
  10.0 180.9 %all-reduce.9.cloned.1.call-start = ((), (), s32[]{:S(2)}) async-start(), calls=%async_computation.4 | async-start | bytes 9437184
  57.4 8.0 %copy-start.2 = (bf16[32,12,3072]{2,1,0:T(8,128)(2,1)S(1)}, bf16[32,12,3072]{2,1,0:T(8,128)(2,1)}, u32[]{:S(2)}) copy-start(bf16[32,12,3072]{2,1,0:T(8,128)(2,1)} %all-gather.11.cloned.1.call-done) | copy-start | bytes 7077892
  78.8 0.9 copy-start
  78.8 0.9 copy-start.4
  78.8 120.9 %copy-start.1 = (f32[1,3072]{1,0:T(1,128)S(1)}, f32[1,3072]{1,0:T(1,128)}, u32[]{:S(2)}) copy-start(f32[1,3072]{1,0:T(1,128)} %param.8) | copy-start | bytes 36868
  78.8 166.5 %all-gather.13.cloned.1.call-start = ((), (), s32[]{:S(2)}) async-start(), calls=%async_computation.1 | async-start | bytes 3244032 | tf_op jit(solution)/shard_map/all_gather | solution.py:49
  193.0 6.5 collective-permute-start
  200.4 178.6 %all-reduce.11.cloned.1.call-start = ((), (), s32[]{:S(2)}) async-start(), calls=%async_computation.5 | async-start | bytes 9437184
  245.3 8.0 %copy-start.3 = (bf16[32,12,3072]{2,1,0:T(8,128)(2,1)S(1)}, bf16[32,12,3072]{2,1,0:T(8,128)(2,1)}, u32[]{:S(2)}) copy-start(bf16[32,12,3072]{2,1,0:T(8,128)(2,1)} %all-gather.13.cloned.1.call-done) | copy-start | bytes 7077892
  266.8 166.7 %all-gather.15.cloned.1.call-start = ((), (), s32[]{:S(2)}) async-start(), calls=%async_computation.2 | async-start | bytes 3244032 | tf_op jit(solution)/shard_map/all_gather | solution.py:49
  381.1 6.5 collective-permute-start.1
  388.5 176.6 %all-reduce.13.cloned.1.call-start = ((), (), s32[]{:S(2)}) async-start(), calls=%async_computation.6 | async-start | bytes 9437184
  452.8 166.7 %all-gather.17.cloned.1.call-start = ((), (), s32[]{:S(2)}) async-start(), calls=%async_computation.3 | async-start | bytes 3244032 | tf_op jit(solution)/shard_map/all_gather | solution.py:49
  567.1 6.5 collective-permute-start.2
  574.5 176.7 %all-reduce.15.cloned.1.call-start = ((), (), s32[]{:S(2)}) async-start(), calls=%async_computation.7 | async-start | bytes 9437184
Sparse Core Ops, SparseCore 0:
  10.1 47.2 all-gather.10
  79.0 111.9 all-reduce.8
  200.6 44.7 all-gather.12
  266.9 112.0 all-reduce.10
  388.6 44.7 all-gather.14
  452.9 112.0 all-reduce.12
  574.7 44.7 all-gather.16
  638.9 112.2 all-reduce.14

commit v2 on v1

--- a/solution.py
+++ b/solution.py
@@ -46,9 +46,11 @@
         if tick > 0:
             current = passed_along(result, "section", 1)
         normed = rms_norm(current, gain_row)
-        gathered = lax.all_gather(normed, "fsdp", axis=0, tiled=False)
+        spread = jnp.broadcast_to(normed[None], (shards,) + normed.shape)
+        gathered = lax.all_to_all(spread, "fsdp", 0, 0, tiled=True)
         partial_value = expert_mix(gathered, coef, gate_w, up_w, down_w)
-        mixed = lax.psum_scatter(partial_value, "fsdp", scatter_dimension=0, tiled=True)[0]
+        pieces = lax.all_to_all(partial_value, "fsdp", 0, 0, tiled=True)
+        mixed = jnp.sum(pieces, axis=0)
         result = (current.astype(jnp.float32) + mixed).astype(jnp.bfloat16)
         output = jnp.where(section_index == tick, result, output)
     return output.reshape(1, micro, local, width)

time: 762 us -> 655 us (0.86)
  the two profiles are of different devices: /device:TPU:24 before, /device:TPU:48 now
where the time goes in v2:
time: 655 us; the launch traced here: 646 us
  blocking collectives  362 us (55%)
  waiting for transfers between devices  135 us (21%)
  matrix products  80.4 us (12%)
  local copies, waits for them, and re-layouts  29 us (4%)
  starting transfers between devices  23.8 us (4%)
  other arithmetic  15.4 us (2%)
    all_to_all x3, blocking collectives, on_device(): pieces = lax.all_to_all(partial_value, 'fsdp', 0, 0, tiled=True)  231 us
    all_to_all x3, blocking collectives, on_device(): gathered = lax.all_to_all(spread, 'fsdp', 0, 0, tiled=True)  131 us
    all_to_all x1, waiting for transfers between devices, on_device(): pieces = lax.all_to_all(partial_value, 'fsdp', 0, 0, tiled=True)  87.1 us
    dot_general x4, matrix products, expert_mix(): jnp.einsum('efmh,ehd->fmd', gated, down_w, preferred_element_type=jnp.flo...  51.9 us
    all_to_all x1, waiting for transfers between devices, on_device(): gathered = lax.all_to_all(spread, 'fsdp', 0, 0, tiled=True)  38.5 us
    dot_general x4, matrix products, expert_mix(): jnp.einsum('fmd,edh->efmh', rows, gate_w, preferred_element_type=jnp.floa...  28.5 us
    dot_general x4, local copies, waits for them, and re-layouts, expert_mix(): jnp.einsum('efmh,ehd->fmd', gated, down_w, preferred_element_type=jnp.flo...  23.3 us
  transfers between devices with their start and end apart: 5, of which 5 were waited for; matrix products, arithmetic and copies ran while one was open for 0% of the time, Pallas kernels for 0%

profile of v2, /device:TPU:48, one launch (start us, length us, event | category | flops | bytes accessed | tf_op | source)
XLA Modules:
  0.0 646.1 jit_solution(10938086799719749543)
XLA Ops:
  0.0 0.9 reshape.94
  0.9 1.0 multiply_reduce_fusion
  1.9 0.1 rsqrt.36
  2.0 0.8 multiply_convert_fusion
  2.8 2.0 broadcast_in_dim.10
  4.9 0.0 copy-start.2
  4.9 0.0 copy-start.3
  4.9 8.2 %all-to-all-start = ((bf16[32,12,3072]{2,1,0:T(8,128)(2,1)}), bf16[32,12,3072]{2,1,0:T(8,128)(2,1)S(1)}, u32[]{:S(2)}, u32[]{:S(2)}) async-start(bf16[32,12,3072]{2,1,0:T(8,128)(2,1)} %broadcast_in_dim.10), calls=%async_computation | async-start | bytes 6291456 | tf_op jit(solution)/shard_map/all_to_all | solution.py:50
  13.0 0.0 copy-done.2
  13.1 0.0 copy-done.3
  13.1 0.2 reshape.92
  13.3 0.7 copy.32
  14.0 38.5 %all-to-all-done = bf16[32,12,3072]{2,1,0:T(8,128)(2,1)S(1)} async-done(((bf16[32,12,3072]{2,1,0:T(8,128)(2,1)}), bf16[32,12,3072]{2,1,0:T(8,128)(2,1)S(1)}, u32[]{:S(2)}, u32[]{:S(2)}) %all-to-all-start) | async-done | bytes 2359328 | tf_op jit(solution)/shard_map/all_to_all | solution.py:50
  52.5 0.0 copy-start.1
  52.5 7.1 %fusion.22 = f32[32,12,4,256]{3,0,2,1:T(8,128)} fusion(bf16[1,4,3072,256]{3,2,1,0:T(8,128)(2,1)} %param.9, bf16[32,12,3072,1]{2,1,0,3:T(8,128)(2,1)S(1)} %bitcast.173), kind=kOutput, calls=%fused_computation.22 | convolution fusion | flops 2415919104 | bytes 10223616 | tf_op jit(solution)/shard_map/fmd,edh->efmh/dot_general | solution.py:29
  59.7 0.0 copy-done.1
  59.7 12.9 %fusion.24 = f32[32,12,3072]{2,0,1:T(8,128)} fusion(bf16[1,4,256,3072]{3,2,1,0:T(8,128)(2,1)} %param.11, f32[32,12,4,256]{3,0,2,1:T(8,128)} %fusion.22, bf16[1,4,3072,256]{3,2,1,0:T(8,128)(2,1)} %param.10, bf16[32,12,3072,1]{2,1,0,3:T(8,128)(2,1)S(1)} %bitcast.174, f32[4,32,12]{1,0,2:T(4,128)S(1)} %bitcast.187), kind=kOutput, calls=%fused_computation.24 | convolution fusion | flops 4834590720 | bytes 21239808 | tf_op jit(solution)/shard_map/efmh,ehd->fmd/dot_general | solution.py:32
  72.6 5.2 copy.33
  77.8 76.9 %all_to_all.40 = f32[32,12,3072]{2,1,0:T(8,128)} all-to-all(f32[32,12,3072]{2,1,0:T(8,128)S(1)} %copy.33), channel_id=1, replica_groups=mesh['section'=4,'fsdp'=32] {'fsdp'}, dimensions={0} | all-to-all | bytes 9437184 | tf_op jit(solution)/shard_map/all_to_all | solution.py:52
  154.7 0.0 copy-start
  154.7 3.2 reduce_sum.83
  157.9 3.2 collective-permute-start
  161.1 3.3 collective-permute-done
  164.4 0.1 fusion.104
  164.6 0.0 copy-done
  164.6 0.1 fusion.106
  164.7 0.4 broadcast_in_dim.11
  165.0 43.8 %all_to_all.41 = bf16[32,12,3072]{2,1,0:T(8,128)(2,1)S(1)} all-to-all(bf16[32,12,3072]{2,1,0:T(8,128)(2,1)S(1)} %broadcast_in_dim.11), channel_id=1, replica_groups=mesh['section'=4,'fsdp'=32] {'fsdp'}, dimensions={0} | all-to-all | bytes 4718592 | tf_op jit(solution)/shard_map/all_to_all | solution.py:50
  208.8 7.1 %fusion.20 = f32[32,12,4,256]{3,0,2,1:T(8,128)} fusion(bf16[1,4,3072,256]{3,2,1,0:T(8,128)(2,1)} %param.9, bf16[32,12,3072,1]{2,1,0,3:T(8,128)(2,1)S(1)} %bitcast.177), kind=kOutput, calls=%fused_computation.20 | convolution fusion | flops 2415919104 | bytes 10223616 | tf_op jit(solution)/shard_map/fmd,edh->efmh/dot_general | solution.py:29
  215.9 12.9 %fusion.27 = f32[32,12,3072]{2,0,1:T(8,128)} fusion(bf16[1,4,256,3072]{3,2,1,0:T(8,128)(2,1)} %param.11, f32[32,12,4,256]{3,0,2,1:T(8,128)} %fusion.20, bf16[1,4,3072,256]{3,2,1,0:T(8,128)(2,1)} %param.10, bf16[32,12,3072,1]{2,1,0,3:T(8,128)(2,1)S(1)} %bitcast.178, f32[4,32,12]{1,0,2:T(4,128)S(1)} %bitcast.188), kind=kOutput, calls=%fused_computation.25 | convolution fusion | flops 4834590720 | bytes 21239808 | tf_op jit(solution)/shard_map/efmh,ehd->fmd/dot_general | solution.py:32
  228.9 5.2 copy.36
  234.0 76.9 %all_to_all.42 = f32[32,12,3072]{2,1,0:T(8,128)} all-to-all(f32[32,12,3072]{2,1,0:T(8,128)S(1)} %copy.36), channel_id=1, replica_groups=mesh['section'=4,'fsdp'=32] {'fsdp'}, dimensions={0} | all-to-all | bytes 9437184 | tf_op jit(solution)/shard_map/all_to_all | solution.py:52
  311.0 3.2 reduce_sum.85
  314.2 3.2 collective-permute-start.1
  317.4 3.3 collective-permute-done.1
  320.7 0.1 fusion.108
  320.9 0.1 fusion.110
  321.0 0.4 broadcast_in_dim.12
  321.3 43.5 %all_to_all.43 = bf16[32,12,3072]{2,1,0:T(8,128)(2,1)S(1)} all-to-all(bf16[32,12,3072]{2,1,0:T(8,128)(2,1)S(1)} %broadcast_in_dim.12), channel_id=1, replica_groups=mesh['section'=4,'fsdp'=32] {'fsdp'}, dimensions={0} | all-to-all | bytes 4718592 | tf_op jit(solution)/shard_map/all_to_all | solution.py:50
  364.8 7.1 %fusion.18 = f32[32,12,4,256]{3,0,2,1:T(8,128)} fusion(bf16[1,4,3072,256]{3,2,1,0:T(8,128)(2,1)} %param.9, bf16[32,12,3072,1]{2,1,0,3:T(8,128)(2,1)S(1)} %bitcast.179), kind=kOutput, calls=%fused_computation.18 | convolution fusion | flops 2415919104 | bytes 10223616 | tf_op jit(solution)/shard_map/fmd,edh->efmh/dot_general | solution.py:29
  372.0 12.9 %fusion.30 = f32[32,12,3072]{2,0,1:T(8,128)} fusion(bf16[1,4,256,3072]{3,2,1,0:T(8,128)(2,1)} %param.11, f32[32,12,4,256]{3,0,2,1:T(8,128)} %fusion.18, bf16[1,4,3072,256]{3,2,1,0:T(8,128)(2,1)} %param.10, bf16[32,12,3072,1]{2,1,0,3:T(8,128)(2,1)S(1)} %bitcast.180, f32[4,32,12]{1,0,2:T(4,128)S(1)} %bitcast.189), kind=kOutput, calls=%fused_computation.26 | convolution fusion | flops 4834590720 | bytes 21239808 | tf_op jit(solution)/shard_map/efmh,ehd->fmd/dot_general | solution.py:32
  384.9 5.2 copy.39
  390.1 76.9 %all_to_all.44 = f32[32,12,3072]{2,1,0:T(8,128)} all-to-all(f32[32,12,3072]{2,1,0:T(8,128)S(1)} %copy.39), channel_id=1, replica_groups=mesh['section'=4,'fsdp'=32] {'fsdp'}, dimensions={0} | all-to-all | bytes 9437184 | tf_op jit(solution)/shard_map/all_to_all | solution.py:52
  467.0 3.2 reduce_sum.87
  470.2 3.2 collective-permute-start.2
  473.4 3.3 collective-permute-done.2
  476.7 0.1 fusion.112
  476.8 0.1 fusion.114
  476.9 0.4 broadcast_in_dim.13
  477.3 43.6 %all_to_all.45 = bf16[32,12,3072]{2,1,0:T(8,128)(2,1)S(1)} all-to-all(bf16[32,12,3072]{2,1,0:T(8,128)(2,1)S(1)} %broadcast_in_dim.13), channel_id=1, replica_groups=mesh['section'=4,'fsdp'=32] {'fsdp'}, dimensions={0} | all-to-all | bytes 4718592 | tf_op jit(solution)/shard_map/all_to_all | solution.py:50
  520.8 7.1 %fusion.16 = f32[32,12,4,256]{3,0,2,1:T(8,128)} fusion(bf16[1,4,3072,256]{3,2,1,0:T(8,128)(2,1)} %param.9, bf16[32,12,3072,1]{2,1,0,3:T(8,128)(2,1)S(1)} %bitcast.175), kind=kOutput, calls=%fused_computation.16 | convolution fusion | flops 2415919104 | bytes 10223616 | tf_op jit(solution)/shard_map/fmd,edh->efmh/dot_general | solution.py:29
  528.0 13.1 %fusion.33 = f32[32,12,3072]{2,0,1:T(8,128)} fusion(bf16[1,4,256,3072]{3,2,1,0:T(8,128)(2,1)} %param.11, f32[32,12,4,256]{3,0,2,1:T(8,128)} %fusion.16, bf16[1,4,3072,256]{3,2,1,0:T(8,128)(2,1)} %param.10, bf16[32,12,3072,1]{2,1,0,3:T(8,128)(2,1)S(1)} %bitcast.176, f32[4,32,12]{1,0,2:T(4,128)} %bitcast.186), kind=kOutput, calls=%fused_computation.27 | convolution fusion | flops 4834590720 | bytes 21239808 | tf_op jit(solution)/shard_map/efmh,ehd->fmd/dot_general | solution.py:32
  541.1 7.8 %copy.42 = f32[32,12,3072]{2,1,0:T(8,128)} copy(f32[32,12,3072]{2,0,1:T(8,128)} %fusion.33) | data formatting | bytes 9437184 | tf_op jit(solution)/shard_map/efmh,ehd->fmd/dot_general | solution.py:32
  548.9 6.0 all-to-all-start.7
  554.9 87.1 %all-to-all-done.7 = f32[32,12,3072]{2,1,0:T(8,128)} async-done(((f32[32,12,3072]{2,1,0:T(8,128)}), f32[32,12,3072]{2,1,0:T(8,128)}, u32[]{:S(2)}, u32[]{:S(2)}) %all-to-all-start.7) | async-done | bytes 4718624 | tf_op jit(solution)/shard_map/all_to_all | solution.py:52
  642.0 3.2 reduce_sum.89
  645.2 0.7 reshape.93
  (9 shorter events, 0.1 us)
Async XLA Ops:
  4.9 8.2 %copy-start.2 = (f32[1,3,128,2]{2,3,1,0:T(2,128)S(1)}, f32[1,3,128,2]{2,3,1,0:T(2,128)}, u32[]{:S(2)}) copy-start(f32[1,3,128,2]{2,3,1,0:T(2,128)} %param.13) | copy-start | bytes 9220
  4.9 8.2 %copy-start.3 = (s32[1,3,128,2]{2,3,1,0:T(2,128)S(1)}, s32[1,3,128,2]{2,3,1,0:T(2,128)}, u32[]{:S(2)}) copy-start(s32[1,3,128,2]{2,3,1,0:T(2,128)} %param.12) | copy-start | bytes 9220
  4.9 47.7 %all-to-all-start = ((bf16[32,12,3072]{2,1,0:T(8,128)(2,1)}), bf16[32,12,3072]{2,1,0:T(8,128)(2,1)S(1)}, u32[]{:S(2)}, u32[]{:S(2)}) async-start(bf16[32,12,3072]{2,1,0:T(8,128)(2,1)} %broadcast_in_dim.10), calls=%async_computation | async-start | bytes 6291456 | tf_op jit(solution)/shard_map/all_to_all | solution.py:50
  52.5 7.1 %copy-start.1 = (f32[4,32,3,4]{1,0,3,2:T(4,128)S(1)}, f32[4,32,3,4]{1,0,3,2:T(4,128)}, u32[]{:S(2)}) copy-start(f32[4,32,3,4]{1,0,3,2:T(4,128)} %copy.32) | copy-start | bytes 18436
  154.7 9.9 %copy-start = (f32[1,3072]{1,0:T(1,128)S(1)}, f32[1,3072]{1,0:T(1,128)}, u32[]{:S(2)}) copy-start(f32[1,3072]{1,0:T(1,128)} %param.8) | copy-start | bytes 36868
  157.9 6.5 %collective-permute-start = (bf16[12,3072]{1,0:T(8,128)(2,1)S(1)}, bf16[12,3072]{1,0:T(8,128)(2,1)S(1)}, u32[]{:S(2)}, u32[]{:S(2)}) collective-permute-start(bf16[12,3072]{1,0:T(8,128)(2,1)S(1)} %add_convert_fusion), channel_id=1, source_target_pairs={{0,32},{32,64},{64,96},{1,33},{33,65},{65,97},{2,34},{34,66},{66,9... | collective-permute-start | bytes 221192 | tf_op jit(solution)/shard_map/ppermute | solution.py:10
  314.2 6.5 %collective-permute-start.1 = (bf16[12,3072]{1,0:T(8,128)(2,1)S(1)}, bf16[12,3072]{1,0:T(8,128)(2,1)S(1)}, u32[]{:S(2)}, u32[]{:S(2)}) collective-permute-start(bf16[12,3072]{1,0:T(8,128)(2,1)S(1)} %fusion.107), channel_id=1, source_target_pairs={{0,32},{32,64},{64,96},{1,33},{33,65},{65,97},{2,34},{34,66},{66,9... | collective-permute-start | bytes 221192 | tf_op jit(solution)/shard_map/ppermute | solution.py:10
  470.2 6.5 %collective-permute-start.2 = (bf16[12,3072]{1,0:T(8,128)(2,1)S(1)}, bf16[12,3072]{1,0:T(8,128)(2,1)S(1)}, u32[]{:S(2)}, u32[]{:S(2)}) collective-permute-start(bf16[12,3072]{1,0:T(8,128)(2,1)S(1)} %fusion.111), channel_id=1, source_target_pairs={{0,32},{32,64},{64,96},{1,33},{33,65},{65,97},{2,34},{34,66},{66,9... | collective-permute-start | bytes 221192 | tf_op jit(solution)/shard_map/ppermute | solution.py:10
  548.9 93.1 %all-to-all-start.7 = ((f32[32,12,3072]{2,1,0:T(8,128)}), f32[32,12,3072]{2,1,0:T(8,128)}, u32[]{:S(2)}, u32[]{:S(2)}) async-start(f32[32,12,3072]{2,1,0:T(8,128)} %copy.42), calls=%async_computation.7 | async-start | bytes 12582912 | tf_op jit(solution)/shard_map/all_to_all | solution.py:52
